TPU v7x, 512 devices: a whole 4x4x16 slice. The times are simulated.
512 devices in a mesh: tiles: 128 (over y, x, z_lo, core), slab: 4 (over z_hi).
Axes of the slice: x: 4, y: 4, z: 16 (z_hi: 4, z_lo: 4; z = z_hi * 4 + z_lo), core: 2. Of those that a mesh axis runs over, the one named last changes fastest.
Arguments:
- adjoint: float32 [4, 3, 512, 8100], P('slab', None, 'tiles'), may hold values from -6 to 6
- state: float32 [4, 3, 512, 8100], P('slab', None, 'tiles'), may hold values from 0.1 to 10
- weights: float32 [4, 512, 8100], P('slab', 'tiles'), may hold values from 0.02 to 0.24
- vertical: float32 [4, 512, 8100], P('slab', 'tiles'), may hold values from 0.02 to 0.3
- mask: int32 [4, 512, 8100], P('slab', 'tiles'), may hold values 0 or 1
- rate: float32 [3, 512, 8100], P(None, 'tiles'), may hold values from 0.005 to 0.1
- neighbours: int32 [512, 4], P('tiles'), may hold values from -1 to 511, as said below
- links: int32 [512, 4], P('tiles'), may hold values from 0 to 7, as said below
- owners: int32 [512], replicated, may hold values from 0 to 127
Outputs:
- adjoint_out: float32 [4, 3, 512, 8100], P('slab', None, 'tiles')
- control_gradient: float32 [4, 128, 675], P('slab', 'tiles')
Inputs may be any that keep to these rules, and one draw needn't show every extreme that they name: Tiles are placed row by row in a layout of 8 columns, tile t at position t + 2: neighbours[t, s] is t - 8, t + 8, t - 1, t + 1 or -1, and links are mutual: if neighbours[t, s] = u >= 0 then neighbours[u, links[t, s] // 2] = t and links[u, links[t, s] // 2] = 2 s + links[t, s] % 2. `links`: 0 where the side is closed; odd only across the seam between the faces and the cap.
All inputs are finite; a program needn't handle non-finite values. No bound on the sum of `mask` on one device may be relied on, other than what follows from the above.
Results may differ from a plain program's by a relative error of at most 0.000071.
Values sent between devices are 32-bit elements; how exact they have to be, the bound alone decides.
A program may use at most 64 MiB of HBM per device.

v0:
```python
import jax
import jax.numpy as jnp
from jax import lax
from jax.sharding import PartitionSpec as P

TILE = 90
SUBSTEPS = 2
BLOCK = 6
ROW_TILES = 8
COARSE = 15


def padded_2(cells, sides, width):
    for axis, dim in sides:
        count = lax.axis_size(axis)
        ends = count - 1
        head = lax.slice_in_dim(cells, 0, width, axis=dim)
        tail = lax.slice_in_dim(cells, cells.shape[dim] - width, cells.shape[dim], axis=dim)
        cells = jnp.concatenate(
            [
                lax.ppermute(tail, axis, [(i, (i + 1) % count) for i in range(ends)]),
                cells,
                lax.ppermute(head, axis, [((i + 1) % count, i) for i in range(ends)]),
            ],
            axis=dim,
        )
    return cells


def from_behind(block, axis, distance):
    devices = range(lax.axis_size(axis))
    route = [(i - distance, i) for i in devices if i - distance in devices]
    return lax.ppermute(block, axis, route)


def edge_rows(field):
    return jnp.concatenate(
        (field[..., 0, :], field[..., -1, :], field[..., :, 0], field[..., :, -1]), axis=-1
    )


def pick_halo(edge_all, source, neighbours, links):
    width = edge_all.shape[-1] // 4
    grid = edge_all.reshape(edge_all.shape[:-1] + (4, width))
    picked = grid[..., source, links // 2, :]
    picked = jnp.where((links % 2)[..., None] == 1, picked[..., ::-1], picked)
    return jnp.where(neighbours[..., None] >= 0, picked, jnp.float32(0.0))


def neighbour_sum(field, halo):
    upper = jnp.concatenate((halo[..., 0, :][..., None, :], field[..., :-1, :]), axis=-2)
    lower = jnp.concatenate((field[..., 1:, :], halo[..., 1, :][..., None, :]), axis=-2)
    left_side = jnp.concatenate((halo[..., 2, :][..., :, None], field[..., :, :-1]), axis=-1)
    right_side = jnp.concatenate((field[..., :, 1:], halo[..., 3, :][..., :, None]), axis=-1)
    return upper + lower + left_side + right_side


def reach_offsets(tiles_dev, number):
    found = set()
    for within in range(tiles_dev):
        for stride in (1, -1, ROW_TILES, -ROW_TILES):
            offset = (within + stride) // tiles_dev
            if offset != 0 and abs(offset) < number:
                found.add(offset)
    return sorted(found)


def window_slots(neighbours, offsets, tiles_dev, here):
    target = jnp.maximum(neighbours, 0)
    moved = target // tiles_dev - here
    slot = jnp.zeros_like(target)
    for number, offset in enumerate(offsets):
        slot = slot + (moved == offset).astype(jnp.int32) * (number + 1)
    return slot * tiles_dev + target % tiles_dev


def shards(adjoint, state, weights, vertical, mask, rate, neighbours, links, owners):
    levels_here, tracers, count_here, cells = adjoint.shape
    shape_four = (levels_here, count_here, TILE, TILE)
    lam = adjoint.reshape(levels_here, tracers, count_here, TILE, TILE)
    wet = mask.astype(jnp.float32).reshape(shape_four)
    mixing = wet * weights.reshape(shape_four)
    stacked = jnp.stack((vertical.reshape(shape_four), wet))
    padded = padded_2(stacked, (("slab", 1),), 1)
    above = stacked[0] * wet * padded[1, :-2]
    below = padded[0, 2:] * padded[1, 2:] * wet
    uptake = 1.0 - rate.reshape(1, tracers, count_here, TILE, TILE)
    wet_edges = edge_rows(wet)
    here = lax.axis_index("tiles")
    offsets = reach_offsets(count_here, lax.axis_size("tiles"))
    source = window_slots(neighbours, offsets, count_here, here)
    for step in range(SUBSTEPS):
        spread = mixing[:, None] * lam
        spread_edges = edge_rows(spread)
        wet_column = wet_edges[:, None]
        spread_parts = [spread_edges]
        wet_parts = [wet_column]
        for offset in offsets:
            moved_spread, moved_wet = from_behind((spread_edges, wet_column), "tiles", -offset)
            spread_parts.append(moved_spread)
            wet_parts.append(moved_wet)
        spread_all = jnp.concatenate(spread_parts, axis=2)
        wet_all = jnp.concatenate(wet_parts, axis=2)
        count = neighbour_sum(wet, pick_halo(wet_all[:, 0], source, neighbours, links))
        halo = pick_halo(spread_all, source, neighbours, links)
        horizontal = lam * (1.0 - (mixing * count)[:, None]) + wet[:, None] * neighbour_sum(
            spread, halo
        )
        taken = horizontal * uptake
        outer = padded_2(taken, (("slab", 0),), 1)
        lam = taken + above[:, None] * (outer[:-2] - taken) + below[:, None] * (outer[2:] - taken)
    term = wet[:, None] * lam * state.reshape(levels_here, tracers, count_here, TILE, TILE)
    term = term.reshape(levels_here, tracers, count_here, COARSE, BLOCK, COARSE, BLOCK).sum(
        axis=(4, 6)
    )
    term = term.reshape(levels_here, tracers, count_here, COARSE * COARSE)
    owner_count = lax.axis_size("tiles")
    start = here * count_here
    mine = lax.dynamic_slice_in_dim(owners, start, count_here)
    onehot = (mine[:, None] == jnp.arange(owner_count, dtype=jnp.int32)[None, :]).astype(
        jnp.float32
    )
    partial_terms = jnp.einsum("lctq,tk->lkcq", term, onehot, precision=lax.Precision.HIGHEST)
    partial_terms = partial_terms.reshape(levels_here, owner_count, tracers * COARSE * COARSE)
    gradient = lax.psum_scatter(partial_terms, "tiles", scatter_dimension=1, tiled=True)
    return (lam.reshape(levels_here, tracers, count_here, TILE * TILE), gradient)


def solution(mesh):
    placed = (
        P("slab", None, "tiles", None),
        P("slab", None, "tiles", None),
        P("slab", "tiles", None),
        P("slab", "tiles", None),
        P("slab", "tiles", None),
        P(None, "tiles", None),
        P("tiles", None),
        P("tiles", None),
        P(),
    )
    return jax.shard_map(
        shards,
        mesh=mesh,
        in_specs=placed,
        out_specs=(P("slab", None, "tiles", None), P("slab", "tiles", None)),
        check_vma=False,
    )
```

profile of v0, /device:TPU:1, one launch (start us, length us, event | category | flops | bytes accessed | tf_op | source)
XLA Modules:
  0.0 1456.9 jit_solution(11280412015304881694)
XLA Ops:
  7.2 0.9 convert_element_type.4
  8.9 4.4 collective-permute-start
  13.2 4.4 collective-permute-start.1
  17.6 2.6 collective-permute-start.2
  20.3 1.3 collective-permute-start.3
  21.8 1.2 squeeze_stack_reshape.3
  23.1 0.7 constant_dynamic-update-slice_fusion.6
  23.8 0.7 constant_dynamic-update-slice_fusion.5
  24.5 8.9 collective-permute-start.8
  33.5 1.1 broadcast_subtract_fusion
  34.7 0.7 fusion.27
  35.4 0.7 fusion.32
  36.4 0.9 sub.65
  37.7 1.2 reshape.556
  38.8 1.9 reshape.554
  41.2 0.6 gather_fusion
  42.5 0.7 copy-done.3
  43.3 0.9 fusion.44
  44.2 0.7 slice_reduce_fusion.3
  45.0 4.2 collective-permute-start.4
  49.2 4.3 collective-permute-start.5
  53.5 1.9 collective-permute-start.6
  55.4 1.3 collective-permute-start.7
  56.7 1.2 fusion.43
  57.9 1.3 collective-permute-start.10
  59.2 0.9 collective-permute-done.7
  60.4 0.6 gather_fusion.1
  61.5 0.3 copy.126
  61.8 1.9 fusion.4
  63.7 0.4 copy.127
  64.0 1.3 collective-permute-start.11
  65.3 15.9 %collective-permute-start.9 = (f32[1,3,4,90,90]{4,2,3,1,0:T(4,128)S(1)}, f32[1,3,4,90,90]{4,2,3,1,0:T(4,128)S(1)}, u32[]{:S(2)}, u32[]{:S(2)}) collective-permute-start(f32[1,3,4,90,90]{4,2,3,1,0:T(4,128)S(1)} %copy.127), channel_id=1, source_target_pairs={{0,1},{1,2},{2,3},{4,5},{5,6},{6,7},{8,9},{9,10},{10,11},{12,13},{... | collective-permute-start | bytes 1166408 | tf_op jit(solution)/shard_map/ppermute | solution.py:21
  81.2 55.9 %collective-permute-done.10 = f32[2,1,4,90,90]{4,3,2,1,0:T(8,128)} collective-permute-done((f32[2,1,4,90,90]{4,3,2,1,0:T(8,128)}, f32[2,1,4,90,90]{4,3,2,1,0:T(8,128)}, u32[]{:S(2)}, u32[]{:S(2)}) %collective-permute-start.10) | collective-permute-done | bytes 259232 | tf_op jit(solution)/shard_map/ppermute | solution.py:23
  137.2 1.3 fusion.20
  138.5 9.9 collective-permute-done.11
  148.4 1.1 broadcast_multiply_fusion
  149.5 1.2 fusion.41
  150.7 0.7 slice_reduce_fusion.1
  151.4 1.3 collective-permute-start.12
  152.7 13.4 collective-permute-start.13
  166.1 1.9 collective-permute-start.14
  168.0 1.3 collective-permute-start.15
  169.3 1.2 fusion.40
  170.5 0.6 collective-permute-done.14
  171.2 1.4 collective-permute-done.15
  172.8 0.6 gather_fusion.2
  173.9 0.3 copy.135
  174.2 2.1 fusion.9
  176.3 0.4 copy.136
  176.7 1.3 collective-permute-start.17
  178.0 9.1 collective-permute-start.16
  187.1 1.9 reshape.562
  189.0 0.8 dynamic_slice.3
  189.8 42.7 %collective-permute-done.17 = f32[1,3,4,90,90]{4,2,3,1,0:T(4,128)S(1)} collective-permute-done((f32[1,3,4,90,90]{4,2,3,1,0:T(4,128)S(1)}, f32[1,3,4,90,90]{4,2,3,1,0:T(4,128)S(1)}, u32[]{:S(2)}, u32[]{:S(2)}) %collective-permute-start.17) | collective-permute-done | bytes 388832 | tf_op jit(solution)/shard_map/ppermute | solution.py:23
  232.5 1.4 multiply_multiply_fusion
  233.9 0.4 copy.140
  234.3 6.3 reshape.563
  240.6 4.4 reduce_sum.9
  245.1 0.5 convolution_bitcast_fusion
  245.7 1.2 copy.143
  246.9 1.3 dynamic-slice
  248.2 1.2 reshape.561
  249.4 1198.9 %all-reduce.3.cloned.1.call-done = f32[1,128,675]{2,0,1:T(1,128)} async-done(((f32[1,128,675]{2,0,1:T(1,128)}), f32[1,128,675]{2,0,1:T(1,128)}) %all-reduce.3.cloned.1.call-update) | async-done | bytes 345616
  1448.3 1.8 dynamic-slice_bitcast_fusion
  (75 shorter events, 4.8 us)
Async XLA Ops:
  7.2 1441.1 %all-reduce.3.cloned.1.call-start = ((), (), s32[]{:S(2)}) async-start(), calls=%async_computation | async-start | bytes 786432
  8.9 31.9 %collective-permute-start = (f32[1,1,4,360]{3,2,1,0:T(4,128)S(1)}, f32[1,1,4,360]{3,2,1,0:T(4,128)S(1)}, u32[]{:S(2)}, u32[]{:S(2)}) collective-permute-start(f32[1,1,4,360]{3,2,1,0:T(4,128)S(1)} %maximum_bitcast_fusion), channel_id=1, source_target_pairs={{0,8},{4,12},{8,16},{12,20},{16,24},{20,28},{24,32},{28,36},{32,40... | collective-permute-start | bytes 17288 | tf_op jit(solution)/shard_map/ppermute | solution.py:33
  13.2 27.7 %collective-permute-start.1 = (f32[1,1,4,360]{3,2,1,0:T(4,128)S(1)}, f32[1,1,4,360]{3,2,1,0:T(4,128)S(1)}, u32[]{:S(2)}, u32[]{:S(2)}) collective-permute-start(f32[1,1,4,360]{3,2,1,0:T(4,128)S(1)} %maximum_bitcast_fusion), channel_id=1, source_target_pairs={{0,4},{4,8},{8,12},{12,16},{16,20},{20,24},{24,28},{28,32},{32,36}... | collective-permute-start | bytes 17288 | tf_op jit(solution)/shard_map/ppermute | solution.py:33
  17.6 23.4 %collective-permute-start.2 = (f32[1,1,4,360]{3,2,1,0:T(4,128)S(1)}, f32[1,1,4,360]{3,2,1,0:T(4,128)S(1)}, u32[]{:S(2)}, u32[]{:S(2)}) collective-permute-start(f32[1,1,4,360]{3,2,1,0:T(4,128)S(1)} %maximum_bitcast_fusion), channel_id=1, source_target_pairs={{4,0},{8,4},{12,8},{16,12},{20,16},{24,20},{28,24},{32,28},{36,32}... | collective-permute-start | bytes 17288 | tf_op jit(solution)/shard_map/ppermute | solution.py:33
  20.3 20.9 %collective-permute-start.3 = (f32[1,1,4,360]{3,2,1,0:T(4,128)S(1)}, f32[1,1,4,360]{3,2,1,0:T(4,128)S(1)}, u32[]{:S(2)}, u32[]{:S(2)}) collective-permute-start(f32[1,1,4,360]{3,2,1,0:T(4,128)S(1)} %maximum_bitcast_fusion), channel_id=1, source_target_pairs={{8,0},{12,4},{16,8},{20,12},{24,16},{28,20},{32,24},{36,28},{40,32... | collective-permute-start | bytes 17288 | tf_op jit(solution)/shard_map/ppermute | solution.py:33
  21.8 14.3 copy-start.1
  23.1 13.0 copy-start.2
  24.5 56.7 %collective-permute-start.8 = (f32[2,1,4,90,90]{4,3,2,1,0:T(8,128)}, f32[2,1,4,90,90]{4,3,2,1,0:T(8,128)}, u32[]{:S(2)}, u32[]{:S(2)}) collective-permute-start(f32[2,1,4,90,90]{4,3,2,1,0:T(8,128)} %constant_dynamic-update-slice_fusion.5), channel_id=1, source_target_pairs={{0,1},{1,2},{2,3},{4,5},{5,6},{6,7},{8,9},{9,10},{10,11},{12,13},{... | collective-permute-start | bytes 777608 | tf_op jit(solution)/shard_map/ppermute | solution.py:21
  42.5 0.7 copy-start.3
  45.0 12.9 collective-permute-start.4
  49.2 10.1 collective-permute-start.5
  53.5 5.8 collective-permute-start.6
  55.4 4.7 collective-permute-start.7
  57.9 79.2 %collective-permute-start.10 = (f32[2,1,4,90,90]{4,3,2,1,0:T(8,128)}, f32[2,1,4,90,90]{4,3,2,1,0:T(8,128)}, u32[]{:S(2)}, u32[]{:S(2)}) collective-permute-start(f32[2,1,4,90,90]{4,3,2,1,0:T(8,128)} %constant_dynamic-update-slice_fusion.5), channel_id=1, source_target_pairs={{1,0},{2,1},{3,2},{5,4},{6,5},{7,6},{9,8},{10,9},{11,10},{13,12},{... | collective-permute-start | bytes 777608 | tf_op jit(solution)/shard_map/ppermute | solution.py:23
  64.0 84.3 %collective-permute-start.11 = (f32[1,3,4,90,90]{4,2,3,1,0:T(4,128)S(1)}, f32[1,3,4,90,90]{4,2,3,1,0:T(4,128)S(1)}, u32[]{:S(2)}, u32[]{:S(2)}) collective-permute-start(f32[1,3,4,90,90]{4,2,3,1,0:T(4,128)S(1)} %copy.127), channel_id=1, source_target_pairs={{1,0},{2,1},{3,2},{5,4},{6,5},{7,6},{9,8},{10,9},{11,10},{13,12},{... | collective-permute-start | bytes 1166408 | tf_op jit(solution)/shard_map/ppermute | solution.py:23
  65.3 83.0 %collective-permute-start.9 = (f32[1,3,4,90,90]{4,2,3,1,0:T(4,128)S(1)}, f32[1,3,4,90,90]{4,2,3,1,0:T(4,128)S(1)}, u32[]{:S(2)}, u32[]{:S(2)}) collective-permute-start(f32[1,3,4,90,90]{4,2,3,1,0:T(4,128)S(1)} %copy.127), channel_id=1, source_target_pairs={{0,1},{1,2},{2,3},{4,5},{5,6},{6,7},{8,9},{9,10},{10,11},{12,13},{... | collective-permute-start | bytes 1166408 | tf_op jit(solution)/shard_map/ppermute | solution.py:21
  138.5 35.7 %copy-start = (f32[4,90,90]{2,1,0:T(8,128)}, f32[4,90,90]{2,1,0:T(8,128)S(1)}, u32[]{:S(2)}) copy-start(f32[4,90,90]{2,1,0:T(8,128)S(1)} %get-tuple-element.35) | copy-start | bytes 388804
  151.4 19.1 %collective-permute-start.12 = (f32[1,3,4,360]{3,2,1,0:T(4,128)S(1)}, f32[1,3,4,360]{3,2,1,0:T(4,128)S(1)}, u32[]{:S(2)}, u32[]{:S(2)}) collective-permute-start(f32[1,3,4,360]{3,2,1,0:T(4,128)S(1)} %pad_maximum_fusion.1), channel_id=1, source_target_pairs={{0,8},{4,12},{8,16},{12,20},{16,24},{20,28},{24,32},{28,36},{32,40... | collective-permute-start | bytes 51848 | tf_op jit(solution)/shard_map/ppermute | solution.py:33
  152.7 17.8 %collective-permute-start.13 = (f32[1,3,4,360]{3,2,1,0:T(4,128)S(1)}, f32[1,3,4,360]{3,2,1,0:T(4,128)S(1)}, u32[]{:S(2)}, u32[]{:S(2)}) collective-permute-start(f32[1,3,4,360]{3,2,1,0:T(4,128)S(1)} %pad_maximum_fusion.1), channel_id=1, source_target_pairs={{0,4},{4,8},{8,12},{12,16},{16,20},{20,24},{24,28},{28,32},{32,36}... | collective-permute-start | bytes 51848 | tf_op jit(solution)/shard_map/ppermute | solution.py:33
  166.1 5.1 collective-permute-start.14
  168.0 4.5 collective-permute-start.15
  176.7 55.8 %collective-permute-start.17 = (f32[1,3,4,90,90]{4,2,3,1,0:T(4,128)S(1)}, f32[1,3,4,90,90]{4,2,3,1,0:T(4,128)S(1)}, u32[]{:S(2)}, u32[]{:S(2)}) collective-permute-start(f32[1,3,4,90,90]{4,2,3,1,0:T(4,128)S(1)} %copy.136), channel_id=1, source_target_pairs={{1,0},{2,1},{3,2},{5,4},{6,5},{7,6},{9,8},{10,9},{11,10},{13,12},{... | collective-permute-start | bytes 1166408 | tf_op jit(solution)/shard_map/ppermute | solution.py:23
  178.0 54.5 %collective-permute-start.16 = (f32[1,3,4,90,90]{4,2,3,1,0:T(4,128)S(1)}, f32[1,3,4,90,90]{4,2,3,1,0:T(4,128)}, u32[]{:S(2)}, u32[]{:S(2)}) collective-permute-start(f32[1,3,4,90,90]{4,2,3,1,0:T(4,128)S(1)} %copy.136), channel_id=1, source_target_pairs={{0,1},{1,2},{2,3},{4,5},{5,6},{6,7},{8,9},{9,10},{10,11},{12,13},{... | collective-permute-start | bytes 1166408 | tf_op jit(solution)/shard_map/ppermute | solution.py:21
Sparse Core Ops, SparseCore 0:
  247.1 1201.1 all-reduce.2
where the time goes:
time: 1460 us
  waiting for transfers between devices  1310 us (90%)
  starting transfers between devices  79.9 us (5%)
  local copies, waits for them, and re-layouts  35.3 us (2%)
  other arithmetic  16.3 us (1%)
    unnamed x2, waiting for transfers between devices  1200 us
    ppermute x3, waiting for transfers between devices, padded_2(): lax.ppermute(head, axis, [((i + 1) % count, i) for i in range(ends)])  109 us
    ppermute x12, starting transfers between devices, from_behind(): return lax.ppermute(block, axis, route)  42.2 us
    ppermute x3, starting transfers between devices, padded_2(): lax.ppermute(tail, axis, [(i, (i + 1) % count) for i in range(ends)])  33.8 us
  transfers between devices with their start and end apart: 19, of which 7 were waited for; matrix products, arithmetic and copies ran while one was open for 2% of the time, Pallas kernels for 0%

commit v1 on v0

v1 whole, which is shorter than its diff:
```python
import jax
import jax.numpy as jnp
from jax import lax
from jax.experimental import pallas as pl
from jax.experimental.pallas import tpu as pltpu
from jax.sharding import PartitionSpec as P

TILE = 90
CELLS = TILE * TILE
SUBSTEPS = 2
BLOCK = 6
COARSE = 15
LANES = 128
ROWS = 64
LEVELS = 4
TRACERS = 3
FULL = LEVELS * ROWS
TAIL = CELLS - (ROWS - 1) * LANES
MESH = pl.DeviceIdType.MESH
FIELDS = 5
LAM = (1, 3, 4)
NEAR = 8
FAR = 16


def iota(shape, dim):
    return lax.broadcasted_iota(jnp.int32, shape, dim)


def shifted(field, distance):
    rows = field.shape[0]
    lane = iota(field.shape, 1)
    down, over = divmod(distance, LANES)
    turned = pltpu.roll(field, (LANES - over) % LANES, 1)
    near = pltpu.roll(turned, (-down) % rows, 0) if down % rows else turned
    far = pltpu.roll(turned, (-down - 1) % rows, 0) if (down + 1) % rows else turned
    return jnp.where(lane >= LANES - over, far, near)


def pieces(value):
    high = value.astype(jnp.bfloat16)
    rest = value - high.astype(jnp.float32)
    middle = rest.astype(jnp.bfloat16)
    low = (rest - middle.astype(jnp.float32)).astype(jnp.bfloat16)
    return high, middle, low


def pick(value, onehot):
    high, middle, low = pieces(value)
    return (
        jnp.dot(high, onehot, preferred_element_type=jnp.float32)
        + jnp.dot(middle, onehot, preferred_element_type=jnp.float32)
        + jnp.dot(low, onehot, preferred_element_type=jnp.float32)
    )


def spread_rows(rows):
    return jnp.concatenate(
        [jnp.broadcast_to(rows[l : l + 1], (ROWS, LANES)) for l in range(LEVELS)], axis=0
    )


def kernel(
    adjoint, state, weights, vertical, mask, rate, neighbours, links, owners,
    out, gradient,
    mine, column, uptake, forward, wet_rows, above_rows, below_rows, keep_rows,
    lam_rows, gather_side, mask_side, place_side, gather_block, mask_block,
    edge_out, edge_in, back_out, back_in, block_own, block_all, part, part_in,
    send_field, recv_field, send_edge, recv_edge, send_back, recv_back,
    send_near, recv_near, send_far, recv_far,
):
    here = lax.axis_index("tiles")
    slab = lax.axis_index("slab")
    tiles = lax.axis_size("tiles")
    core = here % 2
    depth = (here // 2) % 4
    across = (here // 8) % 4
    along = here // 32

    def slab_peer(k):
        return here, (slab + k) % LEVELS

    def beside(n):
        if n == 0:
            return (here + tiles - 2) % tiles, slab
        if n == 1:
            return (here + 2) % tiles, slab
        if n == 2:
            gone = (slab == 0).astype(jnp.int32)
            return (here + tiles - gone) % tiles, (slab + LEVELS - 1) % LEVELS
        gone = (slab == LEVELS - 1).astype(jnp.int32)
        return (here + gone) % tiles, (slab + 1) % LEVELS

    near_me = across * 2 + core
    far_me = along * 4 + depth

    def near_peer(k):
        other = (near_me + k) % NEAR
        return along * 32 + (other // 2) * 8 + depth * 2 + other % 2, slab

    def far_peer(k):
        other = (far_me + k) % FAR
        return (other // 4) * 32 + across * 8 + (other % 4) * 2 + core, slab

    barrier = pltpu.get_barrier_semaphore()
    peers = (
        [slab_peer(k) for k in range(1, LEVELS)]
        + [beside(n) for n in range(4)]
        + [near_peer(k) for k in range(1, NEAR)]
        + [far_peer(k) for k in range(1, FAR)]
    )
    for peer in peers:
        pl.semaphore_signal(barrier, inc=1, device_id=peer, device_id_type=MESH)

    small = iota((4, LANES), 1) < TAIL

    def last(ref, *lead):
        tail = ref[(*lead, slice(None), slice(CELLS - LANES, CELLS))]
        return jnp.where(small, pltpu.roll(tail, TAIL, 1), jnp.zeros_like(tail))

    def load_all(start, read, read_last, target):
        def body(k, carry):
            target[pl.ds(start + k, 4, stride=ROWS), :] = read(pl.ds(pl.multiple_of(k * LANES, LANES), LANES))
            return carry

        lax.fori_loop(0, ROWS - 1, body, 0)
        target[pl.ds(start + ROWS - 1, 4, stride=ROWS), :] = read_last()

    def wet_of(value):
        return value.astype(jnp.float32)

    load_all(
        0,
        lambda at: wet_of(mask[0, :, at]) * weights[0, :, at],
        lambda: wet_of(last(mask, 0)) * last(weights, 0),
        mine,
    )
    load_all(LAM[0] * FULL, lambda at: adjoint[0, 0, :, at], lambda: last(adjoint, 0, 0), mine)
    load_all(
        2 * FULL,
        lambda at: wet_of(mask[0, :, at]) * vertical[0, :, at],
        lambda: wet_of(last(mask, 0)) * last(vertical, 0),
        mine,
    )
    for c in (1, 2):
        load_all(
            LAM[c] * FULL,
            lambda at, c=c: adjoint[0, c, :, at],
            lambda c=c: last(adjoint, 0, c),
            mine,
        )

    pl.semaphore_wait(barrier, len(peers))

    def row_of(f, which):
        return pl.ds(pl.multiple_of(f * FULL + which * ROWS, ROWS), ROWS)

    def field_copy(f, k):
        to = slab_peer(k)
        return pltpu.make_async_remote_copy(
            src_ref=mine.at[row_of(f, to[1])],
            dst_ref=column.at[row_of(f, slab)],
            send_sem=send_field.at[f, k],
            recv_sem=recv_field.at[f, k],
            device_id=to,
            device_id_type=MESH,
        )

    for f in range(FIELDS):
        for k in (1, 3, 2):
            field_copy(f, k).start()
        column[row_of(f, slab), :] = mine[row_of(f, slab), :]

    position = iota((LANES, 2 * LANES), 1)
    y = position % LANES
    cell = TILE * y + jnp.where(position < LANES, 0, TILE - 1)
    lane = iota((LANES, 2 * LANES), 0)
    gather_side[...] = ((cell % LANES == lane) & (y < TILE)).astype(jnp.bfloat16)
    position = iota((ROWS, 2 * LANES), 1)
    y = position % LANES
    cell = TILE * y + jnp.where(position < LANES, 0, TILE - 1)
    mask_side[...] = ((cell // LANES == iota((ROWS, 2 * LANES), 0)) & (y < TILE)).astype(jnp.float32)
    position = iota((2 * LANES, LANES), 0)
    y = position % LANES
    cell = TILE * y + jnp.where(position < LANES, 0, TILE - 1)
    place_side[...] = ((cell % LANES == iota((2 * LANES, LANES), 1)) & (y < TILE)).astype(jnp.bfloat16)
    position = iota((LANES, 2 * LANES), 1)
    cell = BLOCK * TILE * (position // COARSE) + BLOCK * (position % COARSE)
    gather_block[...] = (
        (cell % LANES == iota((LANES, 2 * LANES), 0)) & (position < COARSE * COARSE)
    ).astype(jnp.bfloat16)
    position = iota((ROWS, 2 * LANES), 1)
    cell = BLOCK * TILE * (position // COARSE) + BLOCK * (position % COARSE)
    mask_block[...] = (
        (cell // LANES == iota((ROWS, 2 * LANES), 0)) & (position < COARSE * COARSE)
    ).astype(jnp.float32)
    turn = (iota((LANES, LANES), 0) + iota((LANES, LANES), 1) == TILE - 1).astype(jnp.bfloat16)

    flat = (iota((FULL, LANES), 0) % ROWS) * LANES + iota((FULL, LANES), 1)
    in_row = flat % TILE
    first_row = flat < TILE
    final_row = flat >= CELLS - TILE
    forward[0:FULL] = (in_row != 0).astype(jnp.float32)
    forward[FULL : 2 * FULL] = (in_row != TILE - 1).astype(jnp.float32)

    for c in range(TRACERS):
        load_all(c * FULL, lambda at, c=c: 1.0 - rate[c, :, at], lambda c=c: 1.0 - last(rate, c), uptake)

    tile = here * 4 + slab
    code, turned = [], []
    for side in range(4):
        to = jnp.full((LEVELS, LANES), neighbours[slab, side], jnp.int32)
        link = jnp.full((LEVELS, LANES), links[slab, side], jnp.int32)
        slot = jnp.where(
            to == tile - 8, 0, jnp.where(to == tile + 8, 4, jnp.where(to == tile - 1, 8, 12))
        )
        code.append(jnp.where(to < 0, -1, slot + lax.shift_right_logical(link, 1)))
        turned.append((link & 1) == 1)

    lane4 = iota((LEVELS, LANES), 1)

    def edges_of(field):
        top = jnp.concatenate([field[l * ROWS : l * ROWS + 1] for l in range(LEVELS)], axis=0)
        one = jnp.concatenate([field[l * ROWS + 62 : l * ROWS + 63] for l in range(LEVELS)], axis=0)
        two = jnp.concatenate([field[l * ROWS + 63 : l * ROWS + 64] for l in range(LEVELS)], axis=0)
        low = jnp.where(lane4 < 54, pltpu.roll(one, 54, 1), pltpu.roll(two, 54, 1))
        sides = pick(field, gather_side[...])
        chosen = mask_side[...]
        rows = jnp.concatenate(
            [
                jnp.sum(sides[l * ROWS : (l + 1) * ROWS] * chosen, axis=0, keepdims=True)
                for l in range(LEVELS)
            ],
            axis=0,
        )
        return top, low, rows[:, :LANES], rows[:, LANES:]

    def edge_copy(m, n):
        return pltpu.make_async_remote_copy(
            src_ref=edge_out.at[m],
            dst_ref=edge_in.at[m, n ^ 1],
            send_sem=send_edge.at[m, n],
            recv_sem=recv_edge.at[m, n ^ 1],
            device_id=beside(n),
            device_id_type=MESH,
        )

    def send_edges(m, field):
        for side, rows in enumerate(edges_of(field)):
            edge_out[m, side * LEVELS : (side + 1) * LEVELS, :] = rows
        for n in range(4):
            edge_copy(m, n).start()

    def halo(m):
        for n in range(4):
            edge_copy(m, n ^ 1).wait_recv()
        found = []
        for side in range(4):
            value = jnp.zeros((LEVELS, LANES), jnp.float32)
            for n in range(4):
                for other in range(4):
                    value = jnp.where(
                        code[side] == n * 4 + other,
                        edge_in[m, n, other * LEVELS : (other + 1) * LEVELS, :],
                        value,
                    )
            found.append(value)
        back = pick(jnp.concatenate(found, axis=0), turn)
        return [
            jnp.where(turned[side], back[side * LEVELS : (side + 1) * LEVELS], found[side])
            for side in range(4)
        ]

    def neighbour_sum(field, m):
        top, low, left, right = halo(m)
        upper = jnp.where(first_row, spread_rows(top), shifted(field, -TILE))
        lower = jnp.where(final_row, spread_rows(pltpu.roll(low, 74, 1)), shifted(field, TILE))
        before = forward[0:FULL] * shifted(field, -1)
        after = forward[FULL : 2 * FULL] * shifted(field, 1)
        chosen = mask_side[...]
        both = jnp.concatenate([left, right], axis=1)
        placed = jnp.concatenate([chosen * both[l : l + 1] for l in range(LEVELS)], axis=0)
        return upper + lower + before + after + pick(placed, place_side[...])

    def arrived(f):
        for k in range(1, LEVELS):
            field_copy(f, k).wait_recv()

    def back_copy(c, k):
        to = slab_peer(k)
        return pltpu.make_async_remote_copy(
            src_ref=back_out.at[row_of(c, to[1])],
            dst_ref=back_in.at[row_of(c, slab)],
            send_sem=send_back.at[c, k],
            recv_sem=recv_back.at[c, k],
            device_id=to,
            device_id_type=MESH,
        )

    def fluxes(c, step):
        m = c * SUBSTEPS + step
        lam = column[LAM[c] * FULL : (LAM[c] + 1) * FULL] if step == 0 else lam_rows[...]
        mixing = column[0:FULL]
        moved = lam * keep_rows[...] + wet_rows[...] * neighbour_sum(mixing * lam, m)
        kept = uptake[row_of(c, slab), :]
        u = jnp.concatenate([moved[l * ROWS : (l + 1) * ROWS] * kept for l in range(LEVELS)], axis=0)
        up = pltpu.roll(u, ROWS, 0)
        down = pltpu.roll(u, FULL - ROWS, 0)
        return u + above_rows[...] * (up - u) + below_rows[...] * (down - u)

    def middle(c):
        lam = fluxes(c, 0)
        lam_rows[...] = lam
        send_edges(c * SUBSTEPS + 1, column[0:FULL] * lam)

    def ends(c):
        lam = fluxes(c, 1)
        back_out[c * FULL : (c + 1) * FULL] = lam
        for k in (1, 3, 2):
            back_copy(c, k).start()
        back_in[row_of(c, slab), :] = back_out[row_of(c, slab), :]

    def opens(c):
        arrived(LAM[c])
        send_edges(c * SUBSTEPS, column[0:FULL] * column[LAM[c] * FULL : (LAM[c] + 1) * FULL])

    arrived(0)
    wet = (column[0:FULL] > 0).astype(jnp.float32)
    wet_rows[...] = wet
    send_edges(TRACERS * SUBSTEPS, wet)
    opens(0)
    keep_rows[...] = 1.0 - column[0:FULL] * neighbour_sum(wet_rows[...], TRACERS * SUBSTEPS)
    arrived(2)
    wet = wet_rows[...]
    inner = iota((FULL, LANES), 0) >= ROWS
    above = jnp.where(inner, column[2 * FULL : 3 * FULL] * pltpu.roll(wet, ROWS, 0), 0.0)
    above_rows[...] = above
    below_rows[...] = pltpu.roll(above, FULL - ROWS, 0)
    middle(0)
    opens(1)
    ends(0)
    middle(1)
    opens(2)
    ends(1)
    middle(2)
    ends(2)

    wide = iota((4, LANES), 1)
    block_own[...] = jnp.zeros_like(block_own)
    for c in range(TRACERS):
        load_all(c * FULL, lambda at, c=c: state[0, c, :, at], lambda c=c: last(state, 0, c), forward_state(forward))
    for c in range(TRACERS):
        for k in range(1, LEVELS):
            back_copy(c, k).wait_recv()

        def body(k, carry, c=c):
            out[0, c, :, pl.ds(pl.multiple_of(k * LANES, LANES), LANES)] = back_in[
                pl.ds(c * FULL + k, 4, stride=ROWS), :
            ]
            return carry

        lax.fori_loop(0, ROWS - 1, body, 0)
        out[0, c, :, (ROWS - 1) * LANES : CELLS] = back_in[
            pl.ds(c * FULL + ROWS - 1, 4, stride=ROWS), :
        ][:, :TAIL]
        lam = back_in[c * FULL : (c + 1) * FULL]
        term = jnp.where(mine[0:FULL] > 0, lam, 0.0) * forward[(2 + c) * FULL : (3 + c) * FULL]
        three = term + shifted(term, 1) + shifted(term, 2)
        six = three + shifted(three, 3)
        three = six + shifted(six, TILE) + shifted(six, 2 * TILE)
        six = three + shifted(three, 3 * TILE)
        blocks = pick(six, gather_block[...])
        chosen = mask_block[...]
        for j in range(4):
            row = jnp.sum(blocks[j * ROWS : (j + 1) * ROWS] * chosen, axis=0, keepdims=True)
            block_own[8 * j + 2 * c : 8 * j + 2 * c + 1, :] = row[:, :LANES]
            block_own[8 * j + 2 * c + 1 : 8 * j + 2 * c + 2, :] = row[:, LANES:]

    def near_copy(k):
        return pltpu.make_async_remote_copy(
            src_ref=block_own,
            dst_ref=block_all.at[near_me],
            send_sem=send_near.at[k],
            recv_sem=recv_near.at[k],
            device_id=near_peer(k),
            device_id_type=MESH,
        )

    for k in range(1, NEAR):
        near_copy(k).start()
    block_all[near_me] = block_own[...]
    which = iota((8 * FAR, LANES), 0) // 8
    owner_of = (which // 4) * 32 + across * 8 + (which % 4) * 2 + core
    for k in range(1, NEAR):
        near_copy(k).wait_recv()

    def add(t, total):
        member = t // 4
        source = along * 32 + (member // 2) * 8 + depth * 2 + member % 2
        owner = jnp.full((8 * FAR, LANES), owners[source * 4 + t % 4], jnp.int32)
        rows = block_all[member, pl.ds(pl.multiple_of((t % 4) * 8, 8), 8), :]
        return total + jnp.where(owner == owner_of, jnp.concatenate([rows] * FAR, axis=0), 0.0)

    part[...] = lax.fori_loop(0, 4 * NEAR, add, jnp.zeros((8 * FAR, LANES), jnp.float32))

    def far_copy(k):
        other = (far_me + k) % FAR
        return pltpu.make_async_remote_copy(
            src_ref=part.at[pl.ds(pl.multiple_of(other * 8, 8), 8)],
            dst_ref=part_in.at[far_me],
            send_sem=send_far.at[k],
            recv_sem=recv_far.at[k],
            device_id=far_peer(k),
            device_id_type=MESH,
        )

    for k in range(1, FAR):
        far_copy(k).start()
    part_in[far_me] = part[pl.ds(pl.multiple_of(far_me * 8, 8), 8), :]
    for k in range(1, FAR):
        far_copy(k).wait_recv()
    total = part_in[0]
    for k in range(1, FAR):
        total = total + part_in[k]
    area = COARSE * COARSE
    for c in range(TRACERS):
        gradient[0, :, c * area : c * area + LANES] = total[2 * c : 2 * c + 1]
        gradient[0, :, c * area + LANES : (c + 1) * area] = total[2 * c + 1 : 2 * c + 2, : area - LANES]

    for f in range(FIELDS):
        for k in range(1, LEVELS):
            field_copy(f, k).wait_send()
    for m in range(TRACERS * SUBSTEPS + 1):
        for n in range(4):
            edge_copy(m, n).wait_send()
    for c in range(TRACERS):
        for k in range(1, LEVELS):
            back_copy(c, k).wait_send()
    for k in range(1, NEAR):
        near_copy(k).wait_send()
    for k in range(1, FAR):
        far_copy(k).wait_send()


def forward_state(ref):
    return ref.at[pl.ds(2 * FULL, TRACERS * FULL)]


def shards(adjoint, state, weights, vertical, mask, rate, neighbours, links, owners):
    vmem = pl.BlockSpec(memory_space=pltpu.VMEM)
    smem = pl.BlockSpec(memory_space=pltpu.SMEM)
    f32 = jnp.float32
    dma = pltpu.SemaphoreType.DMA
    edges = TRACERS * SUBSTEPS + 1
    return pl.pallas_call(
        kernel,
        out_shape=(
            jax.ShapeDtypeStruct(adjoint.shape, f32),
            jax.ShapeDtypeStruct((1, 1, TRACERS * COARSE * COARSE), f32),
        ),
        in_specs=[vmem] * 6 + [smem] * 3,
        out_specs=(vmem, vmem),
        scratch_shapes=[
            pltpu.VMEM((FIELDS * FULL, LANES), f32),
            pltpu.VMEM((FIELDS * FULL, LANES), f32),
            pltpu.VMEM((TRACERS * FULL, LANES), f32),
            pltpu.VMEM((5 * FULL, LANES), f32),
            pltpu.VMEM((FULL, LANES), f32),
            pltpu.VMEM((FULL, LANES), f32),
            pltpu.VMEM((FULL, LANES), f32),
            pltpu.VMEM((FULL, LANES), f32),
            pltpu.VMEM((FULL, LANES), f32),
            pltpu.VMEM((LANES, 2 * LANES), jnp.bfloat16),
            pltpu.VMEM((ROWS, 2 * LANES), f32),
            pltpu.VMEM((2 * LANES, LANES), jnp.bfloat16),
            pltpu.VMEM((LANES, 2 * LANES), jnp.bfloat16),
            pltpu.VMEM((ROWS, 2 * LANES), f32),
            pltpu.VMEM((edges, 4 * LEVELS, LANES), f32),
            pltpu.VMEM((edges, 4, 4 * LEVELS, LANES), f32),
            pltpu.VMEM((TRACERS * FULL, LANES), f32),
            pltpu.VMEM((TRACERS * FULL, LANES), f32),
            pltpu.VMEM((32, LANES), f32),
            pltpu.VMEM((NEAR, 32, LANES), f32),
            pltpu.VMEM((8 * FAR, LANES), f32),
            pltpu.VMEM((FAR, 8, LANES), f32),
            dma((FIELDS, LEVELS)),
            dma((FIELDS, LEVELS)),
            dma((edges, 4)),
            dma((edges, 4)),
            dma((TRACERS, LEVELS)),
            dma((TRACERS, LEVELS)),
            dma((NEAR,)),
            dma((NEAR,)),
            dma((FAR,)),
            dma((FAR,)),
        ],
        compiler_params=pltpu.CompilerParams(
            collective_id=0, has_side_effects=True, vmem_limit_bytes=48 << 20
        ),
    )(adjoint, state, weights, vertical, mask, rate, neighbours, links, owners)


def solution(mesh):
    placed = (
        P("slab", None, "tiles", None),
        P("slab", None, "tiles", None),
        P("slab", "tiles", None),
        P("slab", "tiles", None),
        P("slab", "tiles", None),
        P(None, "tiles", None),
        P("tiles", None),
        P("tiles", None),
        P(),
    )
    return jax.shard_map(
        shards,
        mesh=mesh,
        in_specs=placed,
        out_specs=(P("slab", None, "tiles", None), P("slab", "tiles", None)),
        check_vma=False,
    )
```

time: 1460 us -> 109 us (0.07)
  waiting for transfers between devices: 1310 us -> 0 us
  Pallas kernels: 0 us -> 98.5 us
  starting transfers between devices: 79.9 us -> 0 us
  local copies, waits for them, and re-layouts: 35.3 us -> 9.06 us
  other arithmetic: 16.3 us -> 0 us
    unnamed x2 -> x0, waiting for transfers between devices: 1200 us -> none
    ppermute x18 -> x0, waiting for transfers between devices: 111 us -> none  [the longest x3 109 us: padded_2(): lax.ppermute(head, axis, [((i + 1) % count, i) for i in range(ends)])]
    pallas_call x0 -> x1, Pallas kernels: none -> 98.5 us  [shards(): pl.pallas_call(kernel, out_shape=(jax.ShapeDtypeStruct(adjoint.shape, f32...]
    ppermute x18 -> x0, starting transfers between devices: 79.9 us -> none  [the longest x12 42.2 us: from_behind(): return lax.ppermute(block, axis, route)]
  transfers between devices with their start and end apart: 19 -> 0, of which waited for: 7 -> 0; matrix products, arithmetic and copies ran while one was open for 2% -> 0% of each run, Pallas kernels for 0% -> 0%
where the time goes in v1:
time: 109 us; the launch traced here: 108 us
  Pallas kernels  98.5 us (90%)
  local copies, waits for them, and re-layouts  9.06 us (8%)
    pallas_call x1, Pallas kernels, shards(): pl.pallas_call(kernel, out_shape=(jax.ShapeDtypeStruct(adjoint.shape, f32...  98.5 us
    unnamed x20, local copies, waits for them, and re-layouts  9.06 us

profile of v1, /device:TPU:1, one launch (start us, length us, event | category | flops | bytes accessed | tf_op | source)
XLA Modules:
  0.0 108.2 jit_solution(13081498734765444910)
XLA Ops:
  0.6 0.0 copy-start
  0.6 1.0 copy-done
  1.6 0.0 copy-start.1
  1.6 1.0 copy-done.1
  2.6 0.0 copy-start.2
  2.6 1.0 copy-done.2
  3.6 0.0 copy-start.3
  3.6 0.9 copy-done.3
  4.5 0.0 copy-start.4
  4.5 0.9 copy-done.4
  5.4 0.0 copy-start.5
  5.4 0.9 copy-done.5
  6.3 0.0 copy-start.6
  6.3 0.7 copy-done.6
  7.0 0.0 copy-start.7
  7.0 0.7 copy-done.7
  7.7 0.0 copy-start.8
  7.7 0.7 copy-done.8
  8.4 98.5 %shard_map.104 = (f32[1,3,4,8100]{3,2,1,0:T(4,128)S(1)}, f32[1,1,675]{2,1,0:T(1,128)S(1)}) custom-call(f32[1,3,4,8100]{3,2,1,0:T(4,128)S(1)} %copy-done, f32[1,3,4,8100]{3,2,1,0:T(4,128)S(1)} %copy-done.1, f32[1,4,8100]{2,1,0:T(4,128)S(1)} %copy-done.3, f32[1,4,8100]{2,1,0:T(4,128)S(1)} %copy-done.4, s32[1,4,8100]{2,1,0:T(4,128)S(1)} %copy-done.5, ...), custom_call_target="tpu_custom_call" | custom-call | tf_op jit(solution)/shard_map/pallas_call | solution.py:455
  106.9 0.7 copy.13
  107.6 0.6 copy.14
Async XLA Ops:
  0.6 1.0 copy-start
  1.6 1.0 copy-start.1
  2.6 1.0 copy-start.2
  3.6 0.9 copy-start.3
  4.5 0.9 copy-start.4
  5.4 0.9 copy-start.5
  6.3 0.7 copy-start.6
  7.0 0.7 copy-start.7
  7.7 0.7 copy-start.8

commit v2 on v1

--- a/solution.py
+++ b/solution.py
@@ -7,7 +7,6 @@
 
 TILE = 90
 CELLS = TILE * TILE
-SUBSTEPS = 2
 BLOCK = 6
 COARSE = 15
 LANES = 128
@@ -18,7 +17,8 @@
 TAIL = CELLS - (ROWS - 1) * LANES
 MESH = pl.DeviceIdType.MESH
 FIELDS = 5
-LAM = (1, 3, 4)
+LAM = 2
+GROUP = 7
 NEAR = 8
 FAR = 16
 
@@ -63,10 +63,13 @@
 def kernel(
     adjoint, state, weights, vertical, mask, rate, neighbours, links, owners,
     out, gradient,
-    mine, column, uptake, forward, wet_rows, above_rows, below_rows, keep_rows,
+    adjoint_in, state_in, weights_in, vertical_in, mask_in, rate_in, neighbours_in, links_in,
+    out_own, owners_in,
+    mine, column, uptake, state_rows, inside, wet_rows, above_rows, below_rows, keep_rows,
     lam_rows, gather_side, mask_side, place_side, gather_block, mask_block,
-    edge_out, edge_in, back_out, back_in, block_own, block_all, part, part_in,
-    send_field, recv_field, send_edge, recv_edge, send_back, recv_back,
+    home_out, home_in, edge_out, edge_in, back_out, back_in, block_own, block_all, part, part_in,
+    fetch, leave,
+    send_field, recv_field, send_home, recv_home, send_edge, recv_edge, send_back, recv_back,
     send_near, recv_near, send_far, recv_far,
 ):
     here = lax.axis_index("tiles")
@@ -91,6 +94,9 @@
         gone = (slab == LEVELS - 1).astype(jnp.int32)
         return (here + gone) % tiles, (slab + 1) % LEVELS
 
+    def home_peer(n):
+        return (here + tiles + (-2, 2, -1, 1)[n]) % tiles, slab
+
     near_me = across * 2 + core
     far_me = along * 4 + depth
 
@@ -102,10 +108,23 @@
         other = (far_me + k) % FAR
         return (other // 4) * 32 + across * 8 + (other % 4) * 2 + core, slab
 
+    arrays = (
+        (mask, mask_in), (weights, weights_in), (vertical, vertical_in), (adjoint, adjoint_in),
+        (rate, rate_in), (neighbours, neighbours_in), (links, links_in), (owners, owners_in),
+        (state, state_in),
+    )
+
+    def fetched(a):
+        return pltpu.make_async_copy(arrays[a][0], arrays[a][1], fetch.at[a])
+
+    for a in range(len(arrays)):
+        fetched(a).start()
+
     barrier = pltpu.get_barrier_semaphore()
     peers = (
         [slab_peer(k) for k in range(1, LEVELS)]
-        + [beside(n) for n in range(4)]
+        + [home_peer(n) for n in range(4)]
+        + [beside(n) for n in (2, 3)]
         + [near_peer(k) for k in range(1, NEAR)]
         + [far_peer(k) for k in range(1, FAR)]
     )
@@ -118,39 +137,47 @@
         tail = ref[(*lead, slice(None), slice(CELLS - LANES, CELLS))]
         return jnp.where(small, pltpu.roll(tail, TAIL, 1), jnp.zeros_like(tail))
 
-    def load_all(start, read, read_last, target):
-        def body(k, carry):
-            target[pl.ds(start + k, 4, stride=ROWS), :] = read(pl.ds(pl.multiple_of(k * LANES, LANES), LANES))
+    def load_all(*jobs):
+        def body(i, carry):
+            for g in range(GROUP):
+                k = i * GROUP + g
+                at = pl.ds(pl.multiple_of(k * LANES, LANES), LANES)
+                for start, read, _, target in jobs:
+                    target[pl.ds(start + k, 4, stride=ROWS), :] = read(at)
             return carry
 
-        lax.fori_loop(0, ROWS - 1, body, 0)
-        target[pl.ds(start + ROWS - 1, 4, stride=ROWS), :] = read_last()
+        lax.fori_loop(0, (ROWS - 1) // GROUP, body, 0)
+        for start, _, read_last, target in jobs:
+            target[pl.ds(start + ROWS - 1, 4, stride=ROWS), :] = read_last()
 
     def wet_of(value):
         return value.astype(jnp.float32)
 
+    for a in range(4):
+        fetched(a).wait()
     load_all(
-        0,
-        lambda at: wet_of(mask[0, :, at]) * weights[0, :, at],
-        lambda: wet_of(last(mask, 0)) * last(weights, 0),
-        mine,
-    )
-    load_all(LAM[0] * FULL, lambda at: adjoint[0, 0, :, at], lambda: last(adjoint, 0, 0), mine)
-    load_all(
-        2 * FULL,
-        lambda at: wet_of(mask[0, :, at]) * vertical[0, :, at],
-        lambda: wet_of(last(mask, 0)) * last(vertical, 0),
-        mine,
-    )
-    for c in (1, 2):
-        load_all(
-            LAM[c] * FULL,
-            lambda at, c=c: adjoint[0, c, :, at],
-            lambda c=c: last(adjoint, 0, c),
+        (
+            0,
+            lambda at: wet_of(mask_in[0, :, at]) * weights_in[0, :, at],
+            lambda: wet_of(last(mask_in, 0)) * last(weights_in, 0),
             mine,
-        )
-
-    pl.semaphore_wait(barrier, len(peers))
+        ),
+        (
+            FULL,
+            lambda at: wet_of(mask_in[0, :, at]) * vertical_in[0, :, at],
+            lambda: wet_of(last(mask_in, 0)) * last(vertical_in, 0),
+            mine,
+        ),
+        *[
+            (
+                (LAM + c) * FULL,
+                lambda at, c=c: adjoint_in[0, c, :, at],
+                lambda c=c: last(adjoint_in, 0, c),
+                mine,
+            )
+            for c in range(TRACERS)
+        ],
+    )
 
     def row_of(f, which):
         return pl.ds(pl.multiple_of(f * FULL + which * ROWS, ROWS), ROWS)
@@ -166,8 +193,8 @@
             device_id_type=MESH,
         )
 
-    for f in range(FIELDS):
-        for k in (1, 3, 2):
+    def send_field_on(f):
+        for k in (2, 1, 3):
             field_copy(f, k).start()
         column[row_of(f, slab), :] = mine[row_of(f, slab), :]
 
@@ -200,22 +227,25 @@
     in_row = flat % TILE
     first_row = flat < TILE
     final_row = flat >= CELLS - TILE
-    forward[0:FULL] = (in_row != 0).astype(jnp.float32)
-    forward[FULL : 2 * FULL] = (in_row != TILE - 1).astype(jnp.float32)
-
-    for c in range(TRACERS):
-        load_all(c * FULL, lambda at, c=c: 1.0 - rate[c, :, at], lambda c=c: 1.0 - last(rate, c), uptake)
-
-    tile = here * 4 + slab
-    code, turned = [], []
-    for side in range(4):
-        to = jnp.full((LEVELS, LANES), neighbours[slab, side], jnp.int32)
-        link = jnp.full((LEVELS, LANES), links[slab, side], jnp.int32)
-        slot = jnp.where(
-            to == tile - 8, 0, jnp.where(to == tile + 8, 4, jnp.where(to == tile - 1, 8, 12))
-        )
-        code.append(jnp.where(to < 0, -1, slot + lax.shift_right_logical(link, 1)))
-        turned.append((link & 1) == 1)
+    inside[0:FULL] = (in_row != 0).astype(jnp.float32)
+    inside[FULL : 2 * FULL] = (in_row != TILE - 1).astype(jnp.float32)
+
+    fetched(5).wait()
+    fetched(6).wait()
+
+    def codes(to_all, link_all, tile):
+        code, turned = [], []
+        for side in range(4):
+            to = jnp.broadcast_to(to_all[:, side : side + 1], (4, LANES))
+            link = jnp.broadcast_to(link_all[:, side : side + 1], (4, LANES))
+            slot = jnp.where(
+                to == tile - 8, 0, jnp.where(to == tile + 8, 4, jnp.where(to == tile - 1, 8, 12))
+            )
+            code.append(jnp.where(to < 0, -1, slot + lax.shift_right_logical(link, 1)))
+            turned.append((link & 1) == 1)
+        return code, turned
+
+    home_codes = codes(neighbours_in[...], links_in[...], here * 4 + iota((4, LANES), 0))
 
     lane4 = iota((LEVELS, LANES), 1)
 
@@ -245,38 +275,60 @@
             device_id_type=MESH,
         )
 
+    def home_copy(n):
+        return pltpu.make_async_remote_copy(
+            src_ref=home_out,
+            dst_ref=home_in.at[n ^ 1],
+            send_sem=send_home.at[n],
+            recv_sem=recv_home.at[n ^ 1],
+            device_id=home_peer(n),
+            device_id_type=MESH,
+        )
+
     def send_edges(m, field):
         for side, rows in enumerate(edges_of(field)):
             edge_out[m, side * LEVELS : (side + 1) * LEVELS, :] = rows
         for n in range(4):
             edge_copy(m, n).start()
 
-    def halo(m):
+    def home_edge(m, n, other):
+        at = other * 4
+        if n < 2:
+            return home_in[n, m, at : at + 4, :]
+        if n == 2:
+            return jnp.concatenate([home_in[n, m, at + 3 : at + 4, :], home_out[m, at : at + 3, :]], axis=0)
+        return jnp.concatenate([home_out[m, at + 1 : at + 4, :], home_in[n, m, at : at + 1, :]], axis=0)
+
+    def halo(edge, which):
+        code, turned = which
+        found = [jnp.zeros((4, LANES), jnp.float32)] * 4
         for n in range(4):
-            edge_copy(m, n ^ 1).wait_recv()
-        found = []
-        for side in range(4):
-            value = jnp.zeros((LEVELS, LANES), jnp.float32)
-            for n in range(4):
-                for other in range(4):
-                    value = jnp.where(
-                        code[side] == n * 4 + other,
-                        edge_in[m, n, other * LEVELS : (other + 1) * LEVELS, :],
-                        value,
-                    )
-            found.append(value)
+            for other in range(4):
+                value = edge(n, other)
+                for side in range(4):
+                    found[side] = jnp.where(code[side] == n * 4 + other, value, found[side])
         back = pick(jnp.concatenate(found, axis=0), turn)
         return [
             jnp.where(turned[side], back[side * LEVELS : (side + 1) * LEVELS], found[side])
             for side in range(4)
         ]
 
-    def neighbour_sum(field, m):
-        top, low, left, right = halo(m)
+    def halo_home(m):
+        return halo(lambda n, other: home_edge(m, n, other), home_codes)
+
+    def halo_column(m):
+        for n in range(4):
+            edge_copy(m, n ^ 1).wait_recv()
+        return halo(
+            lambda n, other: edge_in[m, n, other * LEVELS : (other + 1) * LEVELS, :], column_codes
+        )
+
+    def neighbour_sum(field, sides):
+        top, low, left, right = sides
         upper = jnp.where(first_row, spread_rows(top), shifted(field, -TILE))
         lower = jnp.where(final_row, spread_rows(pltpu.roll(low, 74, 1)), shifted(field, TILE))
-        before = forward[0:FULL] * shifted(field, -1)
-        after = forward[FULL : 2 * FULL] * shifted(field, 1)
+        before = inside[0:FULL] * shifted(field, -1)
+        after = inside[FULL : 2 * FULL] * shifted(field, 1)
         chosen = mask_side[...]
         both = jnp.concatenate([left, right], axis=1)
         placed = jnp.concatenate([chosen * both[l : l + 1] for l in range(LEVELS)], axis=0)
@@ -297,74 +349,114 @@
             device_id_type=MESH,
         )
 
-    def fluxes(c, step):
-        m = c * SUBSTEPS + step
-        lam = column[LAM[c] * FULL : (LAM[c] + 1) * FULL] if step == 0 else lam_rows[...]
-        mixing = column[0:FULL]
-        moved = lam * keep_rows[...] + wet_rows[...] * neighbour_sum(mixing * lam, m)
-        kept = uptake[row_of(c, slab), :]
-        u = jnp.concatenate([moved[l * ROWS : (l + 1) * ROWS] * kept for l in range(LEVELS)], axis=0)
+    def couple(u):
         up = pltpu.roll(u, ROWS, 0)
         down = pltpu.roll(u, FULL - ROWS, 0)
         return u + above_rows[...] * (up - u) + below_rows[...] * (down - u)
 
-    def middle(c):
-        lam = fluxes(c, 0)
-        lam_rows[...] = lam
-        send_edges(c * SUBSTEPS + 1, column[0:FULL] * lam)
-
-    def ends(c):
-        lam = fluxes(c, 1)
-        back_out[c * FULL : (c + 1) * FULL] = lam
-        for k in (1, 3, 2):
-            back_copy(c, k).start()
-        back_in[row_of(c, slab), :] = back_out[row_of(c, slab), :]
-
-    def opens(c):
-        arrived(LAM[c])
-        send_edges(c * SUBSTEPS, column[0:FULL] * column[LAM[c] * FULL : (LAM[c] + 1) * FULL])
-
+    for c in range(TRACERS):
+        lam = mine[(LAM + c) * FULL : (LAM + c + 1) * FULL]
+        for side, rows in enumerate(edges_of(mine[0:FULL] * lam)):
+            home_out[c, side * 4 : (side + 1) * 4, :] = rows
+    for side, rows in enumerate(edges_of((mine[0:FULL] > 0).astype(jnp.float32))):
+        home_out[TRACERS, side * 4 : (side + 1) * 4, :] = rows
+
+    pl.semaphore_wait(barrier, len(peers))
+    for n in range(4):
+        home_copy(n).start()
+    send_field_on(0)
+    send_field_on(1)
+
+    fetched(4).wait()
+    load_all(
+        *[
+            (c * FULL, lambda at, c=c: 1.0 - rate_in[c, :, at], lambda c=c: 1.0 - last(rate_in, c), uptake)
+            for c in range(TRACERS)
+        ]
+    )
+    for n in range(4):
+        home_copy(n ^ 1).wait_recv()
+    wet = (mine[0:FULL] > 0).astype(jnp.float32)
+    wet_rows[...] = wet
+    keep_rows[...] = 1.0 - mine[0:FULL] * neighbour_sum(wet, halo_home(TRACERS))
+    for c in range(TRACERS):
+        lam = mine[(LAM + c) * FULL : (LAM + c + 1) * FULL]
+        moved = lam * keep_rows[...] + wet_rows[...] * neighbour_sum(mine[0:FULL] * lam, halo_home(c))
+        mine[(LAM + c) * FULL : (LAM + c + 1) * FULL] = moved * uptake[c * FULL : (c + 1) * FULL]
+        send_field_on(LAM + c)
+
+    column_codes = codes(
+        jnp.broadcast_to(neighbours_in[pl.ds(slab, 1), :], (4, 4)),
+        jnp.broadcast_to(links_in[pl.ds(slab, 1), :], (4, 4)),
+        here * 4 + slab,
+    )
     arrived(0)
     wet = (column[0:FULL] > 0).astype(jnp.float32)
     wet_rows[...] = wet
-    send_edges(TRACERS * SUBSTEPS, wet)
-    opens(0)
-    keep_rows[...] = 1.0 - column[0:FULL] * neighbour_sum(wet_rows[...], TRACERS * SUBSTEPS)
-    arrived(2)
-    wet = wet_rows[...]
+    send_edges(TRACERS, wet)
+    arrived(1)
     inner = iota((FULL, LANES), 0) >= ROWS
-    above = jnp.where(inner, column[2 * FULL : 3 * FULL] * pltpu.roll(wet, ROWS, 0), 0.0)
+    above = jnp.where(inner, column[FULL : 2 * FULL] * pltpu.roll(wet, ROWS, 0), 0.0)
     above_rows[...] = above
     below_rows[...] = pltpu.roll(above, FULL - ROWS, 0)
-    middle(0)
+
+    def opens(c):
+        arrived(LAM + c)
+        at = pl.ds((LAM + c) * FULL, FULL)
+        lam = couple(column[at, :])
+        lam_rows[c * FULL : (c + 1) * FULL] = lam
+        send_edges(c, column[0:FULL] * lam)
+
+    def ends(c):
+        lam = lam_rows[c * FULL : (c + 1) * FULL]
+        moved = lam * keep_rows[...] + wet_rows[...] * neighbour_sum(column[0:FULL] * lam, halo_column(c))
+        kept = uptake[row_of(c, slab), :]
+        u = jnp.concatenate([moved[l * ROWS : (l + 1) * ROWS] * kept for l in range(LEVELS)], axis=0)
+        back_out[c * FULL : (c + 1) * FULL] = couple(u)
+        for k in (2, 1, 3):
+            back_copy(c, k).start()
+        back_in[row_of(c, slab), :] = back_out[row_of(c, slab), :]
+
+    opens(0)
+    keep_rows[...] = 1.0 - column[0:FULL] * neighbour_sum(wet_rows[...], halo_column(TRACERS))
     opens(1)
     ends(0)
-    middle(1)
     opens(2)
     ends(1)
-    middle(2)
     ends(2)
 
-    wide = iota((4, LANES), 1)
+    fetched(7).wait()
+    fetched(8).wait()
     block_own[...] = jnp.zeros_like(block_own)
-    for c in range(TRACERS):
-        load_all(c * FULL, lambda at, c=c: state[0, c, :, at], lambda c=c: last(state, 0, c), forward_state(forward))
+    load_all(
+        *[
+            (c * FULL, lambda at, c=c: state_in[0, c, :, at], lambda c=c: last(state_in, 0, c), state_rows)
+            for c in range(TRACERS)
+        ]
+    )
+
+    def left(c):
+        return pltpu.make_async_copy(out_own.at[c], out.at[0, c], leave.at[c])
+
     for c in range(TRACERS):
         for k in range(1, LEVELS):
             back_copy(c, k).wait_recv()
 
-        def body(k, carry, c=c):
-            out[0, c, :, pl.ds(pl.multiple_of(k * LANES, LANES), LANES)] = back_in[
-                pl.ds(c * FULL + k, 4, stride=ROWS), :
-            ]
+        def body(i, carry, c=c):
+            for g in range(GROUP):
+                k = i * GROUP + g
+                out_own[c, :, pl.ds(pl.multiple_of(k * LANES, LANES), LANES)] = back_in[
+                    pl.ds(c * FULL + k, 4, stride=ROWS), :
+                ]
             return carry
 
-        lax.fori_loop(0, ROWS - 1, body, 0)
-        out[0, c, :, (ROWS - 1) * LANES : CELLS] = back_in[
+        lax.fori_loop(0, (ROWS - 1) // GROUP, body, 0)
+        out_own[c, :, (ROWS - 1) * LANES : CELLS] = back_in[
             pl.ds(c * FULL + ROWS - 1, 4, stride=ROWS), :
         ][:, :TAIL]
+        left(c).start()
         lam = back_in[c * FULL : (c + 1) * FULL]
-        term = jnp.where(mine[0:FULL] > 0, lam, 0.0) * forward[(2 + c) * FULL : (3 + c) * FULL]
+        term = jnp.where(mine[0:FULL] > 0, lam, 0.0) * state_rows[c * FULL : (c + 1) * FULL]
         three = term + shifted(term, 1) + shifted(term, 2)
         six = three + shifted(three, 3)
         three = six + shifted(six, TILE) + shifted(six, 2 * TILE)
@@ -394,14 +486,15 @@
     for k in range(1, NEAR):
         near_copy(k).wait_recv()
 
-    def add(t, total):
-        member = t // 4
+    def add(member, total):
         source = along * 32 + (member // 2) * 8 + depth * 2 + member % 2
-        owner = jnp.full((8 * FAR, LANES), owners[source * 4 + t % 4], jnp.int32)
-        rows = block_all[member, pl.ds(pl.multiple_of((t % 4) * 8, 8), 8), :]
-        return total + jnp.where(owner == owner_of, jnp.concatenate([rows] * FAR, axis=0), 0.0)
-
-    part[...] = lax.fori_loop(0, 4 * NEAR, add, jnp.zeros((8 * FAR, LANES), jnp.float32))
+        for j in range(4):
+            owner = jnp.full((8 * FAR, LANES), owners_in[source * 4 + j], jnp.int32)
+            rows = block_all[member, 8 * j : 8 * j + 8, :]
+            total = total + jnp.where(owner == owner_of, jnp.concatenate([rows] * FAR, axis=0), 0.0)
+        return total
+
+    part[...] = lax.fori_loop(0, NEAR, add, jnp.zeros((8 * FAR, LANES), jnp.float32))
 
     def far_copy(k):
         other = (far_me + k) % FAR
@@ -430,7 +523,9 @@
     for f in range(FIELDS):
         for k in range(1, LEVELS):
             field_copy(f, k).wait_send()
-    for m in range(TRACERS * SUBSTEPS + 1):
+    for n in range(4):
+        home_copy(n).wait_send()
+    for m in range(TRACERS + 1):
         for n in range(4):
             edge_copy(m, n).wait_send()
     for c in range(TRACERS):
@@ -440,51 +535,60 @@
         near_copy(k).wait_send()
     for k in range(1, FAR):
         far_copy(k).wait_send()
-
-
-def forward_state(ref):
-    return ref.at[pl.ds(2 * FULL, TRACERS * FULL)]
+    for c in range(TRACERS):
+        left(c).wait()
 
 
 def shards(adjoint, state, weights, vertical, mask, rate, neighbours, links, owners):
     vmem = pl.BlockSpec(memory_space=pltpu.VMEM)
-    smem = pl.BlockSpec(memory_space=pltpu.SMEM)
+    hbm = pl.BlockSpec(memory_space=pltpu.HBM)
     f32 = jnp.float32
     dma = pltpu.SemaphoreType.DMA
-    edges = TRACERS * SUBSTEPS + 1
+    held = [adjoint, state, weights, vertical, mask, rate, neighbours, links]
+    edges = TRACERS + 1
     return pl.pallas_call(
         kernel,
         out_shape=(
             jax.ShapeDtypeStruct(adjoint.shape, f32),
             jax.ShapeDtypeStruct((1, 1, TRACERS * COARSE * COARSE), f32),
         ),
-        in_specs=[vmem] * 6 + [smem] * 3,
-        out_specs=(vmem, vmem),
-        scratch_shapes=[
+        in_specs=[hbm] * 9,
+        out_specs=(hbm, vmem),
+        scratch_shapes=[pltpu.VMEM(a.shape, a.dtype) for a in held]
+        + [
+            pltpu.VMEM(adjoint.shape[1:], f32),
+            pltpu.SMEM(owners.shape, owners.dtype),
             pltpu.VMEM((FIELDS * FULL, LANES), f32),
             pltpu.VMEM((FIELDS * FULL, LANES), f32),
             pltpu.VMEM((TRACERS * FULL, LANES), f32),
-            pltpu.VMEM((5 * FULL, LANES), f32),
+            pltpu.VMEM((TRACERS * FULL, LANES), f32),
+            pltpu.VMEM((2 * FULL, LANES), f32),
             pltpu.VMEM((FULL, LANES), f32),
             pltpu.VMEM((FULL, LANES), f32),
             pltpu.VMEM((FULL, LANES), f32),
             pltpu.VMEM((FULL, LANES), f32),
-            pltpu.VMEM((FULL, LANES), f32),
+            pltpu.VMEM((TRACERS * FULL, LANES), f32),
             pltpu.VMEM((LANES, 2 * LANES), jnp.bfloat16),
             pltpu.VMEM((ROWS, 2 * LANES), f32),
             pltpu.VMEM((2 * LANES, LANES), jnp.bfloat16),
             pltpu.VMEM((LANES, 2 * LANES), jnp.bfloat16),
             pltpu.VMEM((ROWS, 2 * LANES), f32),
-            pltpu.VMEM((edges, 4 * LEVELS, LANES), f32),
-            pltpu.VMEM((edges, 4, 4 * LEVELS, LANES), f32),
+            pltpu.VMEM((edges, 16, LANES), f32),
+            pltpu.VMEM((4, edges, 16, LANES), f32),
+            pltpu.VMEM((edges, 16, LANES), f32),
+            pltpu.VMEM((edges, 4, 16, LANES), f32),
             pltpu.VMEM((TRACERS * FULL, LANES), f32),
             pltpu.VMEM((TRACERS * FULL, LANES), f32),
             pltpu.VMEM((32, LANES), f32),
             pltpu.VMEM((NEAR, 32, LANES), f32),
             pltpu.VMEM((8 * FAR, LANES), f32),
             pltpu.VMEM((FAR, 8, LANES), f32),
+            dma((9,)),
+            dma((TRACERS,)),
             dma((FIELDS, LEVELS)),
             dma((FIELDS, LEVELS)),
+            dma((4,)),
+            dma((4,)),
             dma((edges, 4)),
             dma((edges, 4)),
             dma((TRACERS, LEVELS)),
@@ -495,7 +599,7 @@
             dma((FAR,)),
         ],
         compiler_params=pltpu.CompilerParams(
-            collective_id=0, has_side_effects=True, vmem_limit_bytes=48 << 20
+            collective_id=0, has_side_effects=True, vmem_limit_bytes=64 << 20
         ),
     )(adjoint, state, weights, vertical, mask, rate, neighbours, links, owners)
 

time: 109 us -> 92.8 us (0.85)
  Pallas kernels: 98.5 us -> 89.6 us
  local copies, waits for them, and re-layouts: 9.06 us -> 2.35 us
    pallas_call x1, Pallas kernels: 98.5 us -> 89.6 us  [shards(): pl.pallas_call(kernel, out_shape=(jax.ShapeDtypeStruct(adjoint.shape, f32...]
    unnamed x20 -> x4, local copies, waits for them, and re-layouts: 9.06 us -> 2.35 us
where the time goes in v2:
time: 92.8 us; the launch traced here: 92.6 us
  Pallas kernels  89.6 us (97%)
  local copies, waits for them, and re-layouts  2.35 us (3%)
    pallas_call x1, Pallas kernels, shards(): pl.pallas_call(kernel, out_shape=(jax.ShapeDtypeStruct(adjoint.shape, f32...  89.6 us
    unnamed x4, local copies, waits for them, and re-layouts  2.35 us

profile of v2, /device:TPU:1, one launch (start us, length us, event | category | flops | bytes accessed | tf_op | source)
XLA Modules:
  0.0 92.6 jit_solution(17007581082444011023)
XLA Ops:
  0.6 89.6 %shard_map.104 = (f32[1,3,4,8100]{3,2,1,0:T(4,128)}, f32[1,1,675]{2,1,0:T(1,128)}) custom-call(f32[1,3,4,8100]{3,2,1,0:T(4,128)} %adjoint.1, f32[1,3,4,8100]{3,2,1,0:T(4,128)} %state.1, f32[1,4,8100]{2,1,0:T(4,128)} %weights.1, f32[1,4,8100]{2,1,0:T(4,128)} %vertical.1, s32[1,4,8100]{2,1,0:T(4,128)} %mask.1, f32[3,4,8100]{2,1,0:T(4,128)} %rate.1, ...), custom_call_target="tpu_custom_call" | custom-call | tf_op jit(solution)/shard_map/pallas_call | solution.py:549
  90.3 0.0 copy-start
  90.3 1.8 %copy.13 = f32[1,3,4,8100]{3,2,1,0:T(4,128)} copy(f32[1,3,4,8100]{3,2,1,0:T(4,128)} %get-tuple-element.4) | data formatting | bytes 777600
  92.1 0.0 copy-done
  92.1 0.6 copy.14
Async XLA Ops:
  90.3 1.8 %copy-start = (f32[1,1,675]{2,1,0:T(1,128)S(1)}, f32[1,1,675]{2,1,0:T(1,128)}, u32[]{:S(2)}) copy-start(f32[1,1,675]{2,1,0:T(1,128)} %get-tuple-element.5) | copy-start | bytes 8104

commit v3 on v2

--- a/solution.py
+++ b/solution.py
@@ -67,9 +67,9 @@
     out_own, owners_in,
     mine, column, uptake, state_rows, inside, wet_rows, above_rows, below_rows, keep_rows,
     lam_rows, gather_side, mask_side, place_side, gather_block, mask_block,
-    home_out, home_in, edge_out, edge_in, back_out, back_in, block_own, block_all, part, part_in,
+    home_out, home_in, wet_out, wet_in, edge_out, edge_in, back_out, back_in, block_own, block_all, part, part_in,
     fetch, leave,
-    send_field, recv_field, send_home, recv_home, send_edge, recv_edge, send_back, recv_back,
+    send_field, recv_field, send_home, recv_home, send_wet, recv_wet, send_edge, recv_edge, send_back, recv_back,
     send_near, recv_near, send_far, recv_far,
 ):
     here = lax.axis_index("tiles")
@@ -193,9 +193,11 @@
             device_id_type=MESH,
         )
 
-    def send_field_on(f):
-        for k in (2, 1, 3):
+    def send_field_on(f, order=(2, 1, 3)):
+        for k in order:
             field_copy(f, k).start()
+
+    def keep_own(f):
         column[row_of(f, slab), :] = mine[row_of(f, slab), :]
 
     position = iota((LANES, 2 * LANES), 1)
@@ -285,9 +287,24 @@
             device_id_type=MESH,
         )
 
+    def wet_copy(k):
+        to = slab_peer(k)
+        return pltpu.make_async_remote_copy(
+            src_ref=wet_out.at[to[1]],
+            dst_ref=wet_in.at[slab],
+            send_sem=send_wet.at[k],
+            recv_sem=recv_wet.at[k],
+            device_id=to,
+            device_id_type=MESH,
+        )
+
+    left_over = LANES - TILE
+
     def send_edges(m, field):
-        for side, rows in enumerate(edges_of(field)):
-            edge_out[m, side * LEVELS : (side + 1) * LEVELS, :] = rows
+        *three, fourth = edges_of(field)
+        for side, rows in enumerate(three):
+            rest = pltpu.roll(fourth, TILE - left_over * side, 1)
+            edge_out[m, side * LEVELS : (side + 1) * LEVELS, :] = jnp.where(lane4 < TILE, rows, rest)
         for n in range(4):
             edge_copy(m, n).start()
 
@@ -319,9 +336,19 @@
     def halo_column(m):
         for n in range(4):
             edge_copy(m, n ^ 1).wait_recv()
-        return halo(
-            lambda n, other: edge_in[m, n, other * LEVELS : (other + 1) * LEVELS, :], column_codes
-        )
+
+        def edge(n, other):
+            if other < 3:
+                return edge_in[m, n, other * LEVELS : (other + 1) * LEVELS, :]
+            parts = [
+                pltpu.roll(edge_in[m, n, p * LEVELS : (p + 1) * LEVELS, :], left_over * (p + 1), 1)
+                for p in range(3)
+            ]
+            return jnp.where(
+                lane4 < left_over, parts[0], jnp.where(lane4 < 2 * left_over, parts[1], parts[2])
+            )
+
+        return halo(edge, column_codes)
 
     def neighbour_sum(field, sides):
         top, low, left, right = sides
@@ -362,10 +389,12 @@
         home_out[TRACERS, side * 4 : (side + 1) * 4, :] = rows
 
     pl.semaphore_wait(barrier, len(peers))
+    send_field_on(0)
     for n in range(4):
         home_copy(n).start()
-    send_field_on(0)
     send_field_on(1)
+    for f in range(2):
+        keep_own(f)
 
     fetched(4).wait()
     load_all(
@@ -378,12 +407,20 @@
         home_copy(n ^ 1).wait_recv()
     wet = (mine[0:FULL] > 0).astype(jnp.float32)
     wet_rows[...] = wet
-    keep_rows[...] = 1.0 - mine[0:FULL] * neighbour_sum(wet, halo_home(TRACERS))
+    sides = halo_home(TRACERS)
+    for side in range(4):
+        for j in range(4):
+            wet_out[j, side : side + 1, :] = sides[side][j : j + 1]
+    for k in (2, 1, 3):
+        wet_copy(k).start()
+    wet_in[slab] = wet_out[slab]
+    keep_rows[...] = 1.0 - mine[0:FULL] * neighbour_sum(wet, sides)
     for c in range(TRACERS):
         lam = mine[(LAM + c) * FULL : (LAM + c + 1) * FULL]
         moved = lam * keep_rows[...] + wet_rows[...] * neighbour_sum(mine[0:FULL] * lam, halo_home(c))
         mine[(LAM + c) * FULL : (LAM + c + 1) * FULL] = moved * uptake[c * FULL : (c + 1) * FULL]
         send_field_on(LAM + c)
+        keep_own(LAM + c)
 
     column_codes = codes(
         jnp.broadcast_to(neighbours_in[pl.ds(slab, 1), :], (4, 4)),
@@ -393,7 +430,6 @@
     arrived(0)
     wet = (column[0:FULL] > 0).astype(jnp.float32)
     wet_rows[...] = wet
-    send_edges(TRACERS, wet)
     arrived(1)
     inner = iota((FULL, LANES), 0) >= ROWS
     above = jnp.where(inner, column[FULL : 2 * FULL] * pltpu.roll(wet, ROWS, 0), 0.0)
@@ -417,8 +453,14 @@
             back_copy(c, k).start()
         back_in[row_of(c, slab), :] = back_out[row_of(c, slab), :]
 
+    for k in range(1, LEVELS):
+        wet_copy(k).wait_recv()
+    sides = [
+        jnp.concatenate([wet_in[l, side : side + 1, :] for l in range(LEVELS)], axis=0)
+        for side in range(4)
+    ]
+    keep_rows[...] = 1.0 - column[0:FULL] * neighbour_sum(wet_rows[...], sides)
     opens(0)
-    keep_rows[...] = 1.0 - column[0:FULL] * neighbour_sum(wet_rows[...], halo_column(TRACERS))
     opens(1)
     ends(0)
     opens(2)
@@ -525,7 +567,9 @@
             field_copy(f, k).wait_send()
     for n in range(4):
         home_copy(n).wait_send()
-    for m in range(TRACERS + 1):
+    for k in range(1, LEVELS):
+        wet_copy(k).wait_send()
+    for m in range(TRACERS):
         for n in range(4):
             edge_copy(m, n).wait_send()
     for c in range(TRACERS):
@@ -575,8 +619,10 @@
             pltpu.VMEM((ROWS, 2 * LANES), f32),
             pltpu.VMEM((edges, 16, LANES), f32),
             pltpu.VMEM((4, edges, 16, LANES), f32),
-            pltpu.VMEM((edges, 16, LANES), f32),
-            pltpu.VMEM((edges, 4, 16, LANES), f32),
+            pltpu.VMEM((4, 8, LANES), f32),
+            pltpu.VMEM((LEVELS, 8, LANES), f32),
+            pltpu.VMEM((TRACERS, 3 * LEVELS, LANES), f32),
+            pltpu.VMEM((TRACERS, 4, 3 * LEVELS, LANES), f32),
             pltpu.VMEM((TRACERS * FULL, LANES), f32),
             pltpu.VMEM((TRACERS * FULL, LANES), f32),
             pltpu.VMEM((32, LANES), f32),
@@ -589,8 +635,10 @@
             dma((FIELDS, LEVELS)),
             dma((4,)),
             dma((4,)),
-            dma((edges, 4)),
-            dma((edges, 4)),
+            dma((LEVELS,)),
+            dma((LEVELS,)),
+            dma((TRACERS, 4)),
+            dma((TRACERS, 4)),
             dma((TRACERS, LEVELS)),
             dma((TRACERS, LEVELS)),
             dma((NEAR,)),

time: 92.8 us -> 92 us (level)
  no operation moved by 1% of the time
where the time goes in v3:
time: 92 us; the launch traced here: 91.8 us
  Pallas kernels  88.8 us (97%)
  local copies, waits for them, and re-layouts  2.35 us (3%)
    pallas_call x1, Pallas kernels, shards(): pl.pallas_call(kernel, out_shape=(jax.ShapeDtypeStruct(adjoint.shape, f32...  88.8 us
    unnamed x4, local copies, waits for them, and re-layouts  2.35 us

profile of v3, /device:TPU:1, one launch (start us, length us, event | category | flops | bytes accessed | tf_op | source)
XLA Modules:
  0.0 91.8 jit_solution(5172990231791310528)
XLA Ops:
  0.6 88.8 %shard_map.104 = (f32[1,3,4,8100]{3,2,1,0:T(4,128)}, f32[1,1,675]{2,1,0:T(1,128)}) custom-call(f32[1,3,4,8100]{3,2,1,0:T(4,128)} %adjoint.1, f32[1,3,4,8100]{3,2,1,0:T(4,128)} %state.1, f32[1,4,8100]{2,1,0:T(4,128)} %weights.1, f32[1,4,8100]{2,1,0:T(4,128)} %vertical.1, s32[1,4,8100]{2,1,0:T(4,128)} %mask.1, f32[3,4,8100]{2,1,0:T(4,128)} %rate.1, ...), custom_call_target="tpu_custom_call" | custom-call | tf_op jit(solution)/shard_map/pallas_call | solution.py:593
  89.5 0.0 copy-start
  89.5 1.8 %copy.13 = f32[1,3,4,8100]{3,2,1,0:T(4,128)} copy(f32[1,3,4,8100]{3,2,1,0:T(4,128)} %get-tuple-element.4) | data formatting | bytes 777600
  91.3 0.0 copy-done
  91.3 0.6 copy.14
Async XLA Ops:
  89.5 1.8 %copy-start = (f32[1,1,675]{2,1,0:T(1,128)S(1)}, f32[1,1,675]{2,1,0:T(1,128)}, u32[]{:S(2)}) copy-start(f32[1,1,675]{2,1,0:T(1,128)} %get-tuple-element.5) | copy-start | bytes 8104

commit v4 on v3

--- a/solution.py
+++ b/solution.py
@@ -67,7 +67,7 @@
     out_own, owners_in,
     mine, column, uptake, state_rows, inside, wet_rows, above_rows, below_rows, keep_rows,
     lam_rows, gather_side, mask_side, place_side, gather_block, mask_block,
-    home_out, home_in, wet_out, wet_in, edge_out, edge_in, back_out, back_in, block_own, block_all, part, part_in,
+    home_out, home_in, end_out, end_in, wet_out, wet_in, edge_out, edge_in, back_out, back_in, block_own, block_all, part, part_in,
     fetch, leave,
     send_field, recv_field, send_home, recv_home, send_wet, recv_wet, send_edge, recv_edge, send_back, recv_back,
     send_near, recv_near, send_far, recv_far,
@@ -277,10 +277,16 @@
             device_id_type=MESH,
         )
 
+    def keep_edge(m, side, rows):
+        home_out[m, side * 4 : (side + 1) * 4, :] = rows
+        at = m * 4 + side
+        end_out[0, at : at + 1, :] = rows[0:1]
+        end_out[1, at : at + 1, :] = rows[3:4]
+
     def home_copy(n):
         return pltpu.make_async_remote_copy(
-            src_ref=home_out,
-            dst_ref=home_in.at[n ^ 1],
+            src_ref=home_out if n < 2 else end_out.at[n - 2],
+            dst_ref=home_in.at[n ^ 1] if n < 2 else end_in.at[(n ^ 1) - 2],
             send_sem=send_home.at[n],
             recv_sem=recv_home.at[n ^ 1],
             device_id=home_peer(n),
@@ -313,8 +319,8 @@
         if n < 2:
             return home_in[n, m, at : at + 4, :]
         if n == 2:
-            return jnp.concatenate([home_in[n, m, at + 3 : at + 4, :], home_out[m, at : at + 3, :]], axis=0)
-        return jnp.concatenate([home_out[m, at + 1 : at + 4, :], home_in[n, m, at : at + 1, :]], axis=0)
+            return jnp.concatenate([end_in[0, m * 4 + other : m * 4 + other + 1, :], home_out[m, at : at + 3, :]], axis=0)
+        return jnp.concatenate([home_out[m, at + 1 : at + 4, :], end_in[1, m * 4 + other : m * 4 + other + 1, :]], axis=0)
 
     def halo(edge, which):
         code, turned = which
@@ -384,9 +390,9 @@
     for c in range(TRACERS):
         lam = mine[(LAM + c) * FULL : (LAM + c + 1) * FULL]
         for side, rows in enumerate(edges_of(mine[0:FULL] * lam)):
-            home_out[c, side * 4 : (side + 1) * 4, :] = rows
+            keep_edge(c, side, rows)
     for side, rows in enumerate(edges_of((mine[0:FULL] > 0).astype(jnp.float32))):
-        home_out[TRACERS, side * 4 : (side + 1) * 4, :] = rows
+        keep_edge(TRACERS, side, rows)
 
     pl.semaphore_wait(barrier, len(peers))
     send_field_on(0)
@@ -480,11 +486,8 @@
     def left(c):
         return pltpu.make_async_copy(out_own.at[c], out.at[0, c], leave.at[c])
 
-    for c in range(TRACERS):
-        for k in range(1, LEVELS):
-            back_copy(c, k).wait_recv()
-
-        def body(i, carry, c=c):
+    def give(c):
+        def body(i, carry):
             for g in range(GROUP):
                 k = i * GROUP + g
                 out_own[c, :, pl.ds(pl.multiple_of(k * LANES, LANES), LANES)] = back_in[
@@ -497,6 +500,13 @@
             pl.ds(c * FULL + ROWS - 1, 4, stride=ROWS), :
         ][:, :TAIL]
         left(c).start()
+
+    for c in range(TRACERS):
+        for k in range(1, LEVELS):
+            back_copy(c, k).wait_recv()
+
+        if c < TRACERS - 1:
+            give(c)
         lam = back_in[c * FULL : (c + 1) * FULL]
         term = jnp.where(mine[0:FULL] > 0, lam, 0.0) * state_rows[c * FULL : (c + 1) * FULL]
         three = term + shifted(term, 1) + shifted(term, 2)
@@ -523,6 +533,7 @@
     for k in range(1, NEAR):
         near_copy(k).start()
     block_all[near_me] = block_own[...]
+    give(TRACERS - 1)
     which = iota((8 * FAR, LANES), 0) // 8
     owner_of = (which // 4) * 32 + across * 8 + (which % 4) * 2 + core
     for k in range(1, NEAR):
@@ -618,7 +629,9 @@
             pltpu.VMEM((LANES, 2 * LANES), jnp.bfloat16),
             pltpu.VMEM((ROWS, 2 * LANES), f32),
             pltpu.VMEM((edges, 16, LANES), f32),
-            pltpu.VMEM((4, edges, 16, LANES), f32),
+            pltpu.VMEM((2, edges, 16, LANES), f32),
+            pltpu.VMEM((2, 16, LANES), f32),
+            pltpu.VMEM((2, 16, LANES), f32),
             pltpu.VMEM((4, 8, LANES), f32),
             pltpu.VMEM((LEVELS, 8, LANES), f32),
             pltpu.VMEM((TRACERS, 3 * LEVELS, LANES), f32),

time: 92 us -> 92.9 us (level)
  Pallas kernels: 88.8 us -> 89.8 us
    pallas_call x1, Pallas kernels: 88.8 us -> 89.8 us  [shards(): pl.pallas_call(kernel, out_shape=(jax.ShapeDtypeStruct(adjoint.shape, f32...]
where the time goes in v4:
time: 92.9 us; the launch traced here: 92.8 us
  Pallas kernels  89.8 us (97%)
  local copies, waits for them, and re-layouts  2.35 us (3%)
    pallas_call x1, Pallas kernels, shards(): pl.pallas_call(kernel, out_shape=(jax.ShapeDtypeStruct(adjoint.shape, f32...  89.8 us
    unnamed x4, local copies, waits for them, and re-layouts  2.35 us

profile of v4, /device:TPU:1, one launch (start us, length us, event | category | flops | bytes accessed | tf_op | source)
XLA Modules:
  0.0 92.8 jit_solution(16538340146435895240)
XLA Ops:
  0.6 89.8 %shard_map.104 = (f32[1,3,4,8100]{3,2,1,0:T(4,128)}, f32[1,1,675]{2,1,0:T(1,128)}) custom-call(f32[1,3,4,8100]{3,2,1,0:T(4,128)} %adjoint.1, f32[1,3,4,8100]{3,2,1,0:T(4,128)} %state.1, f32[1,4,8100]{2,1,0:T(4,128)} %weights.1, f32[1,4,8100]{2,1,0:T(4,128)} %vertical.1, s32[1,4,8100]{2,1,0:T(4,128)} %mask.1, f32[3,4,8100]{2,1,0:T(4,128)} %rate.1, ...), custom_call_target="tpu_custom_call" | custom-call | tf_op jit(solution)/shard_map/pallas_call | solution.py:604
  90.4 0.0 copy-start
  90.4 1.8 %copy.13 = f32[1,3,4,8100]{3,2,1,0:T(4,128)} copy(f32[1,3,4,8100]{3,2,1,0:T(4,128)} %get-tuple-element.4) | data formatting | bytes 777600
  92.2 0.0 copy-done
  92.2 0.6 copy.14
Async XLA Ops:
  90.4 1.8 %copy-start = (f32[1,1,675]{2,1,0:T(1,128)S(1)}, f32[1,1,675]{2,1,0:T(1,128)}, u32[]{:S(2)}) copy-start(f32[1,1,675]{2,1,0:T(1,128)} %get-tuple-element.5) | copy-start | bytes 8104
